TPU v7x, 256 devices: a whole 4x4x8 slice. The times are simulated.
256 devices in a mesh: expert: 32 (over z, y), etp: 8 (over x, core).
Axes of the slice: x: 4, y: 4, z: 8, core: 2. Of those that a mesh axis runs over, the one named last changes fastest.
Arguments:
- tokens: bfloat16 [32768, 2560], P(('expert', 'etp')), may hold values from -6 to 6
- grad_out: bfloat16 [32768, 2560], P(('expert', 'etp')), may hold values from -6 to 6
- router_weight: bfloat16 [2560, 32], replicated, may hold values from -0.125 to 0.125
- expert_choice: int32 [32768, 1], P(('expert', 'etp')), may hold values from 0 to 31; in each aligned block of 128 rows (0 to 127, 128 to 255, ...) at most 6 rows name the same one
- gate_pre: bfloat16 [32, 1536, 4096], P('expert', None, 'etp'), may hold values from -6 to 6
- up_pre: bfloat16 [32, 1536, 4096], P('expert', None, 'etp'), may hold values from -6 to 6
- w_gate: bfloat16 [32, 2560, 4096], P('expert', None, 'etp'), may hold values from -0.125 to 0.125
- w_up: bfloat16 [32, 2560, 4096], P('expert', None, 'etp'), may hold values from -0.125 to 0.125
- w_down: bfloat16 [32, 4096, 2560], P('expert', 'etp'), may hold values from -0.09375 to 0.09375
Outputs:
- token_grad: bfloat16 [32768, 2560], P(('expert', 'etp'))
- router_grad: float32 [2560, 32], replicated
Inputs may be any that keep to these rules, and one draw needn't show every extreme that they name: `expert_choice`: within the 128 tokens of one device no expert is chosen more than 6 times, and in every draw some expert is chosen exactly 6 times by the tokens of some device.
All inputs are finite; a program needn't handle non-finite values.
Results may differ from a plain program's by a relative error of at most 0.015.
Values may be sent and summed in bfloat16 or wider, within the bound.
No kernel may reach another device: no remote copies, remote signals or barrier semaphores. Data moves between devices by JAX's collectives and lax.ppermute only.
A program may use at most 128 MiB of HBM per device.

v0:
```python
import jax
import jax.numpy as jnp
from jax import lax
from jax.sharding import PartitionSpec as P


def local(tokens, grad_out, router_weight, expert_choice, gate_pre, up_pre, w_gate, w_up, w_down):
    width = tokens.shape[1]
    experts = router_weight.shape[1]
    n_expert = lax.axis_size("expert")
    n_etp = lax.axis_size("etp")
    capacity = gate_pre.shape[1] // (n_expert * n_etp)
    contract = (((1,), (1,)), ((), ()))
    chosen_ids = expert_choice[:, 0]
    picked = chosen_ids[:, None] == jnp.arange(experts, dtype=jnp.int32)[None, :]
    logits = jnp.dot(tokens, router_weight, preferred_element_type=jnp.float32)
    score = jax.nn.sigmoid(jnp.sum(jnp.where(picked, logits, 0.0), axis=1))
    counts = picked.astype(jnp.int32)
    earlier = jnp.cumsum(counts, axis=0) - counts
    position = jnp.sum(earlier * counts, axis=1)
    target = chosen_ids * capacity + position
    placed = jnp.arange(experts * capacity, dtype=jnp.int32)[:, None] == target[None, :]
    onehot = placed.astype(jnp.bfloat16)
    outgoing = jnp.dot(onehot, grad_out, preferred_element_type=jnp.float32).astype(jnp.bfloat16)
    own = lax.all_to_all(outgoing, "expert", split_axis=0, concat_axis=0, tiled=True)
    arrived = lax.all_gather(own, "etp", axis=0, tiled=True)
    d_hidden = lax.dot_general(arrived, w_down[0], contract, preferred_element_type=jnp.float32)
    gate_f = gate_pre[0].astype(jnp.float32)
    up_f = up_pre[0].astype(jnp.float32)
    sig = jax.nn.sigmoid(gate_f)
    d_gate = (d_hidden * up_f * sig * (1.0 + gate_f * (1.0 - sig))).astype(jnp.bfloat16)
    d_up = (d_hidden * gate_f * sig).astype(jnp.bfloat16)
    terms = (
        lax.dot_general(d_gate, w_gate[0], contract, preferred_element_type=jnp.float32)
        + lax.dot_general(d_up, w_up[0], contract, preferred_element_type=jnp.float32)
    ).astype(jnp.bfloat16)
    summed = lax.psum_scatter(terms, "etp", scatter_dimension=0, tiled=True)
    returned = lax.all_to_all(summed, "expert", split_axis=0, concat_axis=0, tiled=True)
    fetched = lax.dot_general(
        onehot, returned, (((0,), (0,)), ((), ())), preferred_element_type=jnp.float32
    )
    inputs = tokens.astype(jnp.float32)
    d_logit = jnp.sum(inputs * fetched, axis=1) * score * (1.0 - score)
    column = lax.dot_general(
        picked.astype(jnp.bfloat16), router_weight, contract, preferred_element_type=jnp.float32
    )
    token_grad = (score[:, None] * fetched + d_logit[:, None] * column).astype(jnp.bfloat16)
    weighted = jnp.where(picked, d_logit[:, None], 0.0)
    local_terms = lax.dot_general(
        weighted,
        inputs,
        (((0,), (0,)), ((), ())),
        precision=lax.Precision.HIGHEST,
        preferred_element_type=jnp.float32,
    )
    mine = lax.all_to_all(
        local_terms.reshape(n_etp, experts // n_etp, width),
        "etp",
        split_axis=0,
        concat_axis=0,
        tiled=True,
    )
    mine = jnp.sum(mine, axis=0)
    mine = lax.psum(mine, "expert")
    router_grad = lax.all_gather(mine, "etp", axis=0, tiled=True).T
    return (token_grad, router_grad)


def solution(mesh):
    placed = (
        P(("expert", "etp"), None),
        P(("expert", "etp"), None),
        P(),
        P(("expert", "etp"), None),
        P("expert", None, "etp"),
        P("expert", None, "etp"),
        P("expert", None, "etp"),
        P("expert", None, "etp"),
        P("expert", "etp", None),
    )
    return jax.shard_map(
        local,
        mesh=mesh,
        in_specs=placed,
        out_specs=(P(("expert", "etp"), None), P()),
        check_vma=False,
    )
```

profile of v0, /device:TPU:1, one launch (start us, length us, event | category | flops | bytes accessed | tf_op | source)
XLA Modules:
  0.0 423.1 jit_solution(13606596880845416231)
XLA Ops:
  7.2 0.0 copy-start
  7.2 0.0 all-gather.3.cloned.1.call-start
  7.2 0.8 fusion.29
  8.0 0.1 copy.15
  8.1 0.2 reduce_window_sum.11
  8.3 0.1 copy.16
  8.4 0.7 select_reduce_fusion
  9.1 0.7 multiply_add_fusion
  9.7 2.5 convolution_convert_fusion
  12.2 2.3 all_to_all.19
  14.4 46.0 %all_to_all.29 = bf16[32,6,2560]{2,1,0:T(8,128)(2,1)} all-to-all(bf16[32,6,2560]{2,1,0:T(8,128)(2,1)} %all_to_all.19), channel_id=1, replica_groups=mesh['expert'=32,'etp'=8] {'expert'}, dimensions={0} | all-to-all | bytes 1966080 | tf_op jit(solution)/shard_map/all_to_all | solution.py:25
  60.4 2.3 all_to_all.21
  62.7 0.0 all-gather.3.cloned.1.call-update
  62.7 0.0 reduce-scatter.2.cloned.1.call-start
  62.8 47.8 %all-gather.3.cloned.1.call-done = bf16[1536,2560]{1,0:T(8,128)(2,1)} async-done(((bf16[192,2560]{1,0:T(8,128)(2,1)}), bf16[1536,2560]{1,0:T(8,128)(2,1)}) %all-gather.3.cloned.1.call-update) | async-done | bytes 7864336 | tf_op jit(solution)/shard_map/all_gather | solution.py:26
  110.6 0.0 copy-start.4
  110.6 0.0 copy-start.5
  110.6 7.5 %fusion.14 = f32[1536,512]{1,0:T(8,128)S(1)} fusion(bf16[1536,2560]{1,0:T(8,128)(2,1)} %all-gather.3.cloned.1.call-done, bf16[1,512,2560]{2,1,0:T(8,128)(2,1)} %param.17), kind=kOutput, calls=%fused_computation.21 | convolution fusion | flops 4026531840 | bytes 13631488 | tf_op jit(solution)/shard_map/dot_general | solution.py:27
  118.1 0.0 copy-start.6
  118.1 1.7 copy-done.6
  119.8 0.0 copy-done
  119.8 0.0 copy-done.4
  119.8 0.0 copy-done.5
  119.8 9.8 %fusion.12 = f32[1536,2560]{1,0:T(8,128)} fusion(bf16[1,2560,512]{2,1,0:T(8,128)(2,1)S(1)} %copy-done, f32[1536,512]{1,0:T(8,128)S(1)} %fusion.14, bf16[1,1536,512]{2,1,0:T(8,128)(2,1)S(1)} %copy-done.4, bf16[1,1536,512]{2,1,0:T(8,128)(2,1)S(1)} %copy-done.5), kind=kOutput, calls=%fused_computation.19 | convolution fusion | flops 4035969024 | bytes 24641536 | tf_op jit(solution)/shard_map/dot_general | solution.py:34
  129.6 15.2 %add_convert_fusion = bf16[1536,2560]{1,0:T(8,128)(2,1)} fusion(f32[1536,2560]{1,0:T(8,128)} %fusion.12, bf16[1,2560,512]{2,1,0:T(8,128)(2,1)} %param.16, f32[1536,512]{1,0:T(8,128)} %copy-done.6, bf16[1,1536,512]{2,1,0:T(8,128)(2,1)} %param.13), kind=kOutput, calls=%fused_computation | convolution fusion | flops 4039901184 | bytes 30932992 | tf_op jit(solution)/shard_map/dot_general | solution.py:35
  144.9 0.0 reduce-scatter.2.cloned.1.call-update
  144.9 0.0 copy-start.1
  144.9 0.0 copy-start.2
  144.9 0.0 copy-start.3
  144.9 51.8 %reduce-scatter.2.cloned.1.call-done = bf16[192,2560]{1,0:T(8,128)(2,1)} async-done(((bf16[1536,2560]{1,0:T(8,128)(2,1)}), bf16[192,2560]{1,0:T(8,128)(2,1)}) %reduce-scatter.2.cloned.1.call-update) | async-done | bytes 983056 | tf_op jit(solution)/shard_map/reduce_scatter | solution.py:37
  196.8 2.3 all_to_all.22
  199.0 9.7 %all-to-all-start.1 = ((bf16[32,6,2560]{2,1,0:T(8,128)(2,1)}), bf16[32,6,2560]{2,1,0:T(8,128)(2,1)}, u32[]{:S(2)}, u32[]{:S(2)}) async-start(bf16[32,6,2560]{2,1,0:T(8,128)(2,1)} %all_to_all.22), calls=%async_computation.2 | async-start | bytes 2621440 | tf_op jit(solution)/shard_map/all_to_all | solution.py:38
  208.7 0.0 copy-done.1
  208.7 0.0 copy-done.2
  208.8 0.0 copy-done.3
  208.8 0.3 fusion.23
  209.1 30.4 %all-to-all-done.1 = bf16[32,6,2560]{2,1,0:T(8,128)(2,1)} async-done(((bf16[32,6,2560]{2,1,0:T(8,128)(2,1)}), bf16[32,6,2560]{2,1,0:T(8,128)(2,1)}, u32[]{:S(2)}, u32[]{:S(2)}) %all-to-all-start.1) | async-done | bytes 983072 | tf_op jit(solution)/shard_map/all_to_all | solution.py:38
  239.5 2.2 all_to_all.24
  241.7 2.7 multiply_reduce_fusion
  244.4 1.1 fusion.27
  245.5 1.8 reshape.36
  247.3 7.3 %all-to-all-start.2 = ((f32[8,4,2560]{2,1,0:T(4,128)}), f32[8,4,2560]{2,1,0:T(4,128)S(1)}, u32[]{:S(2)}, u32[]{:S(2)}) async-start(f32[8,4,2560]{2,1,0:T(4,128)} %reshape.36), calls=%async_computation.3 | async-start | bytes 655360 | tf_op jit(solution)/shard_map/all_to_all | solution.py:56
  254.6 2.5 fusion.1
  257.1 4.6 %all-to-all-done.2 = f32[8,4,2560]{2,1,0:T(4,128)S(1)} async-done(((f32[8,4,2560]{2,1,0:T(4,128)}), f32[8,4,2560]{2,1,0:T(4,128)S(1)}, u32[]{:S(2)}, u32[]{:S(2)}) %all-to-all-start.2) | async-done | bytes 327712 | tf_op jit(solution)/shard_map/all_to_all | solution.py:56
  261.7 0.1 reduce_sum.39
  261.8 112.4 %psum.7 = f32[4,2560]{1,0:T(4,128)S(1)} all-reduce(f32[4,2560]{1,0:T(4,128)S(1)} %reduce_sum.39), channel_id=1, replica_groups=mesh['expert'=32,'etp'=8] {'expert'}, use_global_device_ids=true, to_apply=%region_6.7 | all-reduce | flops 10240 | bytes 81920 | tf_op jit(solution)/shard_map/psum | solution.py:64
  374.2 41.3 %all-gather = f32[8,4,2560]{2,1,0:T(4,128)S(1)} all-gather(f32[1,4,2560]{2,1,0:T(4,128)S(1)} %bitcast.37), channel_id=1, replica_groups=mesh['expert'=32,'etp'=8] {'etp'}, dimensions={0}, use_global_device_ids=true | all-gather | bytes 368640 | tf_op jit(solution)/shard_map/all_gather | solution.py:65
  415.5 0.8 reshape.40
  (1 shorter events, 0.0 us)
Async XLA Ops:
  7.2 112.6 %copy-start = (bf16[1,2560,512]{2,1,0:T(8,128)(2,1)S(1)}, bf16[1,2560,512]{2,1,0:T(8,128)(2,1)}, u32[]{:S(2)}) copy-start(bf16[1,2560,512]{2,1,0:T(8,128)(2,1)} %param.15) | copy-start | bytes 7864324
  7.2 103.4 %all-gather.3.cloned.1.call-start = ((), (), s32[]{:S(2)}) async-start(), calls=%async_computation.4 | async-start | bytes 8847360 | tf_op jit(solution)/shard_map/all_gather | solution.py:26
  62.7 134.0 %reduce-scatter.2.cloned.1.call-start = ((), (), s32[]{:S(2)}) async-start(), calls=%async_computation.5 | async-start | bytes 8847360 | tf_op jit(solution)/shard_map/reduce_scatter | solution.py:37
  110.6 9.3 %copy-start.4 = (bf16[1,1536,512]{2,1,0:T(8,128)(2,1)S(1)}, bf16[1,1536,512]{2,1,0:T(8,128)(2,1)}, u32[]{:S(2)}) copy-start(bf16[1,1536,512]{2,1,0:T(8,128)(2,1)} %param.14) | copy-start | bytes 4718596
  110.6 9.3 %copy-start.5 = (bf16[1,1536,512]{2,1,0:T(8,128)(2,1)S(1)}, bf16[1,1536,512]{2,1,0:T(8,128)(2,1)}, u32[]{:S(2)}) copy-start(bf16[1,1536,512]{2,1,0:T(8,128)(2,1)} %param.13) | copy-start | bytes 4718596
  118.1 1.7 copy-start.6
  144.9 63.8 %copy-start.1 = (bf16[128,2560]{1,0:T(8,128)(2,1)S(1)}, bf16[128,2560]{1,0:T(8,128)(2,1)}, u32[]{:S(2)}) copy-start(bf16[128,2560]{1,0:T(8,128)(2,1)} %param.9) | copy-start | bytes 1966084
  144.9 63.8 %copy-start.2 = (bf16[2560,32]{0,1:T(8,128)(2,1)S(1)}, bf16[2560,32]{0,1:T(8,128)(2,1)}, u32[]{:S(2)}) copy-start(bf16[2560,32]{0,1:T(8,128)(2,1)} %param.11) | copy-start | bytes 491524
  144.9 63.8 %copy-start.3 = (s32[128,1]{0,1:T(1,128)S(1)}, s32[128,1]{0,1:T(1,128)}, u32[]{:S(2)}) copy-start(s32[128,1]{0,1:T(1,128)} %param.12) | copy-start | bytes 1540
  199.0 40.4 %all-to-all-start.1 = ((bf16[32,6,2560]{2,1,0:T(8,128)(2,1)}), bf16[32,6,2560]{2,1,0:T(8,128)(2,1)}, u32[]{:S(2)}, u32[]{:S(2)}) async-start(bf16[32,6,2560]{2,1,0:T(8,128)(2,1)} %all_to_all.22), calls=%async_computation.2 | async-start | bytes 2621440 | tf_op jit(solution)/shard_map/all_to_all | solution.py:38
  247.3 14.4 %all-to-all-start.2 = ((f32[8,4,2560]{2,1,0:T(4,128)}), f32[8,4,2560]{2,1,0:T(4,128)S(1)}, u32[]{:S(2)}, u32[]{:S(2)}) async-start(f32[8,4,2560]{2,1,0:T(4,128)} %reshape.36), calls=%async_computation.3 | async-start | bytes 655360 | tf_op jit(solution)/shard_map/all_to_all | solution.py:56
Sparse Core Ops, SparseCore 0:
  62.9 47.6 all-gather.2
  145.0 51.6 reduce-scatter.1
where the time goes:
time: 424 us; the launch traced here: 423 us
  blocking collectives  200 us (47%)
  waiting for transfers between devices  135 us (32%)
  matrix products  41.7 us (10%)
  starting transfers between devices  17.1 us (4%)
  between operations  14.1 us (3%)
  local copies, waits for them, and re-layouts  13.6 us (3%)
    psum x1, blocking collectives, local(): mine = lax.psum(mine, 'expert')  112 us
    reduce_scatter x1, waiting for transfers between devices, local(): summed = lax.psum_scatter(terms, 'etp', scatter_dimension=0, tiled=True)  51.8 us
    all_gather x1, waiting for transfers between devices, local(): arrived = lax.all_gather(own, 'etp', axis=0, tiled=True)  47.8 us
    all_to_all x1, blocking collectives, local(): lax.all_to_all(outgoing, 'expert', split_axis=0, concat_axis=0, tiled=True)  46 us
    all_gather x1, blocking collectives, local(): router_grad = lax.all_gather(mine, 'etp', axis=0, tiled=True).T  41.3 us
    all_to_all x1, waiting for transfers between devices, local(): lax.all_to_all(summed, 'expert', split_axis=0, concat_axis=0, tiled=True)  30.4 us
    dot_general x1, matrix products, local(): lax.dot_general(d_up, w_up[0], contract, preferred_element_type=jnp.float32)  15.2 us
    dot_general x1, matrix products, local(): lax.dot_general(d_gate, w_gate[0], contract, preferred_element_type=jnp.f...  9.81 us
  transfers between devices with their start and end apart: 4, of which 4 were waited for; matrix products, arithmetic and copies ran while one was open for 1% of the time, Pallas kernels for 0%

commit v1 on v0

--- a/solution.py
+++ b/solution.py
@@ -23,7 +23,15 @@
     onehot = placed.astype(jnp.bfloat16)
     outgoing = jnp.dot(onehot, grad_out, preferred_element_type=jnp.float32).astype(jnp.bfloat16)
     own = lax.all_to_all(outgoing, "expert", split_axis=0, concat_axis=0, tiled=True)
-    arrived = lax.all_gather(own, "etp", axis=0, tiled=True)
+    arrived = jnp.concatenate(
+        lax.all_to_all(
+            jnp.stack([own for _ in range(lax.psum(1, "etp"))], axis=0),
+            "etp",
+            split_axis=0,
+            concat_axis=0,
+        ),
+        axis=0,
+    )
     d_hidden = lax.dot_general(arrived, w_down[0], contract, preferred_element_type=jnp.float32)
     gate_f = gate_pre[0].astype(jnp.float32)
     up_f = up_pre[0].astype(jnp.float32)

time: 424 us -> 461 us (1.087)
  blocking collectives: 200 us -> 295 us
  waiting for transfers between devices: 135 us -> 81 us
    all_to_all x0 -> x1, blocking collectives: none -> 95.9 us  [local(): lax.all_to_all(jnp.stack([own for _ in range(lax.psum(1, 'etp'))], axis=0...]
    all_gather x1 -> x0, waiting for transfers between devices: 47.8 us -> none  [local(): arrived = lax.all_gather(own, 'etp', axis=0, tiled=True)]
    reduce_scatter x1, waiting for transfers between devices: 51.8 us -> 46.1 us  [local(): summed = lax.psum_scatter(terms, 'etp', scatter_dimension=0, tiled=True)]
  transfers between devices with their start and end apart: 4 -> 3, of which waited for: 4 -> 3; matrix products, arithmetic and copies ran while one was open for 1% -> 1% of each run, Pallas kernels for 0% -> 0%
where the time goes in v1:
time: 461 us; the launch traced here: 460 us
  blocking collectives  295 us (64%)
  waiting for transfers between devices  81 us (18%)
  matrix products  37.3 us (8%)
  starting transfers between devices  16.9 us (4%)
  between operations  14.2 us (3%)
  local copies, waits for them, and re-layouts  13.5 us (3%)
    psum x1, blocking collectives, local(): mine = lax.psum(mine, 'expert')  112 us
    all_to_all x1, blocking collectives, local(): lax.all_to_all(jnp.stack([own for _ in range(lax.psum(1, 'etp'))], axis=0...  95.9 us
    reduce_scatter x1, waiting for transfers between devices, local(): summed = lax.psum_scatter(terms, 'etp', scatter_dimension=0, tiled=True)  46.1 us
    all_to_all x1, blocking collectives, local(): lax.all_to_all(outgoing, 'expert', split_axis=0, concat_axis=0, tiled=True)  45.9 us
    all_gather x1, blocking collectives, local(): router_grad = lax.all_gather(mine, 'etp', axis=0, tiled=True).T  41.3 us
    all_to_all x1, waiting for transfers between devices, local(): lax.all_to_all(summed, 'expert', split_axis=0, concat_axis=0, tiled=True)  30.4 us
    dot_general x1, matrix products, local(): lax.dot_general(d_up, w_up[0], contract, preferred_element_type=jnp.float32)  15.2 us
    dot_general x1, matrix products, local(): lax.dot_general(d_gate, w_gate[0], contract, preferred_element_type=jnp.f...  9.88 us
  transfers between devices with their start and end apart: 3, of which 3 were waited for; matrix products, arithmetic and copies ran while one was open for 1% of the time, Pallas kernels for 0%

profile of v1, /device:TPU:1, one launch (start us, length us, event | category | flops | bytes accessed | tf_op | source)
XLA Modules:
  0.0 460.5 jit_solution(9700229709786381388)
XLA Ops:
  7.2 0.0 copy-start
  7.2 0.0 reduce-scatter.2.cloned.1.call-start
  7.2 0.8 fusion.29
  8.0 0.1 copy.15
  8.1 0.2 reduce_window_sum.11
  8.3 0.1 copy.16
  8.4 0.7 select_reduce_fusion
  9.1 0.7 multiply_add_fusion
  9.7 2.5 convolution_convert_fusion
  12.2 2.3 all_to_all.20
  14.5 45.9 %all_to_all.31 = bf16[32,6,2560]{2,1,0:T(8,128)(2,1)} all-to-all(bf16[32,6,2560]{2,1,0:T(8,128)(2,1)} %all_to_all.20), channel_id=1, replica_groups=mesh['expert'=32,'etp'=8] {'expert'}, dimensions={0} | all-to-all | bytes 1966080 | tf_op jit(solution)/shard_map/all_to_all | solution.py:25
  60.4 2.2 stack.4
  62.6 1.9 stack.5
  64.5 0.0 copy-start.5
  64.5 95.9 %all_to_all.32 = bf16[8,192,2560]{2,1,0:T(8,128)(2,1)S(1)} all-to-all(bf16[8,192,2560]{2,1,0:T(8,128)(2,1)S(1)} %stack.5), channel_id=1, replica_groups=mesh['expert'=32,'etp'=8] {'etp'}, dimensions={0} | all-to-all | bytes 15728640 | tf_op jit(solution)/shard_map/all_to_all | solution.py:27
  160.5 0.0 copy-done.5
  160.5 0.0 copy-start.6
  160.5 0.0 copy-start.7
  160.5 4.3 fusion.14
  164.8 0.0 copy-start.8
  164.8 1.7 copy-done.8
  166.5 0.0 copy-done
  166.5 0.0 copy-done.6
  166.5 0.0 copy-done.7
  166.5 9.9 %fusion.12 = f32[1536,2560]{1,0:T(8,128)} fusion(bf16[1,2560,512]{2,1,0:T(8,128)(2,1)S(1)} %copy-done, f32[1536,512]{1,0:T(8,128)S(1)} %fusion.14, bf16[1,1536,512]{2,1,0:T(8,128)(2,1)S(1)} %copy-done.6, bf16[1,1536,512]{2,1,0:T(8,128)(2,1)S(1)} %copy-done.7), kind=kOutput, calls=%fused_computation.19 | convolution fusion | flops 4035969024 | bytes 24641536 | tf_op jit(solution)/shard_map/dot_general | solution.py:42
  176.3 15.2 %add_convert_fusion = bf16[1536,2560]{1,0:T(8,128)(2,1)} fusion(f32[1536,2560]{1,0:T(8,128)} %fusion.12, bf16[1,2560,512]{2,1,0:T(8,128)(2,1)} %param.16, f32[1536,512]{1,0:T(8,128)} %copy-done.8, bf16[1,1536,512]{2,1,0:T(8,128)(2,1)} %param.13), kind=kOutput, calls=%fused_computation | convolution fusion | flops 4039901184 | bytes 30932992 | tf_op jit(solution)/shard_map/dot_general | solution.py:43
  191.6 0.0 reduce-scatter.2.cloned.1.call-update
  191.6 0.0 copy-start.2
  191.6 0.0 copy-start.3
  191.6 0.0 copy-start.4
  191.7 46.1 %reduce-scatter.2.cloned.1.call-done = bf16[192,2560]{1,0:T(8,128)(2,1)} async-done(((bf16[1536,2560]{1,0:T(8,128)(2,1)}), bf16[192,2560]{1,0:T(8,128)(2,1)}) %reduce-scatter.2.cloned.1.call-update) | async-done | bytes 983056 | tf_op jit(solution)/shard_map/reduce_scatter | solution.py:45
  237.7 2.3 all_to_all.23
  240.0 9.6 %all-to-all-start.2 = ((bf16[32,6,2560]{2,1,0:T(8,128)(2,1)}), bf16[32,6,2560]{2,1,0:T(8,128)(2,1)S(1)}, u32[]{:S(2)}, u32[]{:S(2)}) async-start(bf16[32,6,2560]{2,1,0:T(8,128)(2,1)} %all_to_all.23), calls=%async_computation.3 | async-start | bytes 2621440 | tf_op jit(solution)/shard_map/all_to_all | solution.py:46
  249.5 0.0 copy-done.2
  249.5 0.0 copy-done.3
  249.6 0.0 copy-done.4
  249.6 0.3 fusion.23
  249.9 30.4 %all-to-all-done.2 = bf16[32,6,2560]{2,1,0:T(8,128)(2,1)S(1)} async-done(((bf16[32,6,2560]{2,1,0:T(8,128)(2,1)}), bf16[32,6,2560]{2,1,0:T(8,128)(2,1)S(1)}, u32[]{:S(2)}, u32[]{:S(2)}) %all-to-all-start.2) | async-done | bytes 983072 | tf_op jit(solution)/shard_map/all_to_all | solution.py:46
  280.3 0.4 all_to_all.25
  280.6 1.5 multiply_reduce_fusion
  282.1 0.0 copy-start.1
  282.1 1.1 fusion.27
  283.2 1.8 reshape.43
  285.0 7.3 %all-to-all-start.3 = ((f32[8,4,2560]{2,1,0:T(4,128)}), f32[8,4,2560]{2,1,0:T(4,128)S(1)}, u32[]{:S(2)}, u32[]{:S(2)}) async-start(f32[8,4,2560]{2,1,0:T(4,128)} %reshape.43), calls=%async_computation.4 | async-start | bytes 655360 | tf_op jit(solution)/shard_map/all_to_all | solution.py:64
  292.3 2.5 fusion.1
  294.9 4.6 all-to-all-done.3
  299.4 0.1 reduce_sum.39
  299.5 112.0 %psum.7 = f32[4,2560]{1,0:T(4,128)S(1)} all-reduce(f32[4,2560]{1,0:T(4,128)S(1)} %reduce_sum.39), channel_id=1, replica_groups=mesh['expert'=32,'etp'=8] {'expert'}, use_global_device_ids=true, to_apply=%region_6.7 | all-reduce | flops 10240 | bytes 81920 | tf_op jit(solution)/shard_map/psum | solution.py:72
  411.5 41.3 %all-gather = f32[8,4,2560]{2,1,0:T(4,128)S(1)} all-gather(f32[1,4,2560]{2,1,0:T(4,128)S(1)} %bitcast.39), channel_id=1, replica_groups=mesh['expert'=32,'etp'=8] {'etp'}, dimensions={0}, use_global_device_ids=true | all-gather | bytes 368640 | tf_op jit(solution)/shard_map/all_gather | solution.py:73
  452.8 0.8 reshape.47
  453.6 0.0 copy-done.1
  (1 shorter events, 0.0 us)
Async XLA Ops:
  7.2 159.3 %copy-start = (bf16[1,2560,512]{2,1,0:T(8,128)(2,1)S(1)}, bf16[1,2560,512]{2,1,0:T(8,128)(2,1)}, u32[]{:S(2)}) copy-start(bf16[1,2560,512]{2,1,0:T(8,128)(2,1)} %param.15) | copy-start | bytes 7864324
  7.2 230.5 %reduce-scatter.2.cloned.1.call-start = ((), (), s32[]{:S(2)}) async-start(), calls=%async_computation.5 | async-start | bytes 8847360 | tf_op jit(solution)/shard_map/reduce_scatter | solution.py:45
  64.5 95.9 %copy-start.5 = (bf16[1,512,2560]{2,1,0:T(8,128)(2,1)S(1)}, bf16[1,512,2560]{2,1,0:T(8,128)(2,1)}, u32[]{:S(2)}) copy-start(bf16[1,512,2560]{2,1,0:T(8,128)(2,1)} %param.17) | copy-start | bytes 7864324
  160.5 6.0 %copy-start.6 = (bf16[1,1536,512]{2,1,0:T(8,128)(2,1)S(1)}, bf16[1,1536,512]{2,1,0:T(8,128)(2,1)}, u32[]{:S(2)}) copy-start(bf16[1,1536,512]{2,1,0:T(8,128)(2,1)} %param.14) | copy-start | bytes 4718596
  160.5 6.0 %copy-start.7 = (bf16[1,1536,512]{2,1,0:T(8,128)(2,1)S(1)}, bf16[1,1536,512]{2,1,0:T(8,128)(2,1)}, u32[]{:S(2)}) copy-start(bf16[1,1536,512]{2,1,0:T(8,128)(2,1)} %param.13) | copy-start | bytes 4718596
  164.8 1.7 copy-start.8
  191.6 57.9 %copy-start.2 = (bf16[128,2560]{1,0:T(8,128)(2,1)S(1)}, bf16[128,2560]{1,0:T(8,128)(2,1)}, u32[]{:S(2)}) copy-start(bf16[128,2560]{1,0:T(8,128)(2,1)} %param.9) | copy-start | bytes 1966084
  191.6 57.9 %copy-start.3 = (bf16[2560,32]{0,1:T(8,128)(2,1)S(1)}, bf16[2560,32]{0,1:T(8,128)(2,1)}, u32[]{:S(2)}) copy-start(bf16[2560,32]{0,1:T(8,128)(2,1)} %param.11) | copy-start | bytes 491524
  191.6 57.9 %copy-start.4 = (s32[128,1]{0,1:T(1,128)S(1)}, s32[128,1]{0,1:T(1,128)}, u32[]{:S(2)}) copy-start(s32[128,1]{0,1:T(1,128)} %param.12) | copy-start | bytes 1540
  240.0 40.3 %all-to-all-start.2 = ((bf16[32,6,2560]{2,1,0:T(8,128)(2,1)}), bf16[32,6,2560]{2,1,0:T(8,128)(2,1)S(1)}, u32[]{:S(2)}, u32[]{:S(2)}) async-start(bf16[32,6,2560]{2,1,0:T(8,128)(2,1)} %all_to_all.23), calls=%async_computation.3 | async-start | bytes 2621440 | tf_op jit(solution)/shard_map/all_to_all | solution.py:46
  282.1 171.5 %copy-start.1 = (bf16[1,2560,512]{2,1,0:T(8,128)(2,1)S(1)}, bf16[1,2560,512]{2,1,0:T(8,128)(2,1)}, u32[]{:S(2)}) copy-start(bf16[1,2560,512]{2,1,0:T(8,128)(2,1)} %param.15) | copy-start | bytes 7864324
  285.0 14.4 %all-to-all-start.3 = ((f32[8,4,2560]{2,1,0:T(4,128)}), f32[8,4,2560]{2,1,0:T(4,128)S(1)}, u32[]{:S(2)}, u32[]{:S(2)}) async-start(f32[8,4,2560]{2,1,0:T(4,128)} %reshape.43), calls=%async_computation.4 | async-start | bytes 655360 | tf_op jit(solution)/shard_map/all_to_all | solution.py:64
Sparse Core Ops, SparseCore 0:
  191.7 45.9 reduce-scatter.1
